TPU v7x, 128 devices: a whole 4x4x4 slice. The times are simulated.
128 devices in a mesh: group: 8 (over y, core), member: 16 (over z, x).
Axes of the slice: x: 4, y: 4, z: 4, core: 2. Of those that a mesh axis runs over, the one named last changes fastest.
Arguments:
- feats: bfloat16 [96, 524288], P(None, ('group', 'member')), may hold values from -6 to 6
- kmap: int32 [27, 524288], P(None, ('group', 'member')), may hold values from 0 to 5888, as said below
- send_rows: int32 [128, 7, 256], P(('group', 'member')), may hold values from 0 to 4095
- w_sub: bfloat16 [27, 96, 96], replicated, may hold values from -0.125 to 0.125
- owner: int32 [524288, 1], P(('group', 'member')), may hold values from 0 to 127, as said below
- coarse_id: int32 [524288], P(('group', 'member')), may hold values from 0 to 511
- octant: int32 [524288], P(('group', 'member')), may hold values from 0 to 7
- w_down: bfloat16 [8, 192, 96], replicated, may hold values from -0.21875 to 0.21875
- grad_coarse: bfloat16 [192, 65536], P(None, ('group', 'member')), may hold values from -6 to 6
Outputs:
- coarse_out: bfloat16 [192, 65536], P(None, ('group', 'member'))
- grad_feats: float32 [96, 524288], P(None, ('group', 'member'))
- grad_w_sub: float32 [27, 96, 96], replicated
- grad_w_down: float32 [8, 192, 96], replicated
Inputs may be any that keep to these rules, and one draw needn't show every extreme that they name: kmap[k, v] indexes the table of v's device: below 4096 a voxel of that device, then 256 received voxels for each of the 7 levels in order, and 5888 for a missing neighbour; kmap[13, v] is v's own column. owner[v, 0] is v's own device or its partner at one of the 7 levels; among the voxels of one device at most 128 name its partner of any one level, and on every device some level's partner is named by exactly 128.
All inputs are finite; a program needn't handle non-finite values.
Results may differ from a plain program's by a relative error of at most 0.0056.
Values may be sent and summed in bfloat16 or wider, within the bound.
No kernel may reach another device: no remote copies, remote signals or barrier semaphores. Data moves between devices by JAX's collectives and lax.ppermute only.
A program may use at most 128 MiB of HBM per device.

v0:
```python
import jax
import jax.numpy as jnp
from jax import lax
from jax.sharding import PartitionSpec as P


def from_partner(value, axis, stride):
    mask = 2**stride
    pairs = [(source, source ^ mask) for source in range(lax.axis_size(axis))]
    return lax.ppermute(value, axis, pairs)


def shards(feats, kmap, send_rows, w_sub, owner, coarse_id, octant, w_down, grad_coarse):
    chans, vdev = feats.shape
    levels = send_rows.shape[1]
    hcap = send_rows.shape[2]
    n_member = lax.axis_size("member")
    bits_member = n_member.bit_length() - 1
    myself = lax.axis_index(("group", "member"))
    outgoing = send_rows[0]
    rows_in = feats.T
    pieces = [jnp.take(rows_in, outgoing[level], axis=0) for level in range(levels)]
    received = []
    for level in range(levels):
        if level < bits_member:
            received.append(from_partner(pieces[level], "member", level))
        else:
            received.append(from_partner(pieces[level], "group", level - bits_member))
    table = jnp.concatenate([rows_in] + received + [jnp.zeros((1, chans), jnp.bfloat16)], axis=0)

    def forward_step(total, inputs):
        weight, cols = inputs
        taken = jnp.take(table, cols, axis=0)
        return (total + jnp.dot(taken, weight.T, preferred_element_type=jnp.float32), None)

    pre, _ = lax.scan(forward_step, jnp.zeros((vdev, chans), jnp.float32), (w_sub, kmap))
    y1 = jax.nn.silu(pre).astype(jnp.bfloat16)
    noct = w_down.shape[0]
    coarse_dev = grad_coarse.shape[1]
    sentinel = noct * coarse_dev
    slots = vdev // 32
    differ = jnp.bitwise_xor(owner[:, 0], myself)
    code = jnp.full((vdev,), levels, jnp.int32)
    for level in range(levels):
        code = jnp.where(differ == 1 << level, level, code)
    classes = (code[None, :] == jnp.arange(levels + 1, dtype=jnp.int32)[:, None]).astype(jnp.int32)
    rank = jnp.sum(classes * (jnp.cumsum(classes, axis=1) - 1), axis=0)
    is_self = code == levels
    position = jnp.where(is_self, levels * slots, code * slots + rank)
    local_keys = octant * coarse_dev + coarse_id
    send_feat = jnp.zeros((levels * slots + 1, chans), jnp.bfloat16).at[position].set(y1)
    send_key = jnp.full((levels * slots + 1,), sentinel, jnp.int32).at[position].set(local_keys)
    got_feats = []
    got_keys = []
    for level in range(levels):
        part_feat = send_feat[level * slots : (level + 1) * slots]
        part_key = send_key[level * slots : (level + 1) * slots]
        if level < bits_member:
            came_feat, came_key = from_partner((part_feat, part_key), "member", level)
        else:
            came_feat, came_key = from_partner((part_feat, part_key), "group", level - bits_member)
        got_feats.append(came_feat)
        got_keys.append(came_key)
    self_keys = jnp.where(is_self, local_keys, sentinel)
    all_keys = jnp.concatenate([self_keys] + got_keys, axis=0)
    all_feats = jnp.concatenate([y1] + got_feats, axis=0)
    pooled = (
        jnp.zeros((sentinel + 1, chans), jnp.float32)
        .at[all_keys]
        .add(all_feats.astype(jnp.float32))
    )
    pooled = pooled[:sentinel].astype(jnp.bfloat16).reshape(noct, coarse_dev, chans)
    coarse_out = jnp.einsum(
        "oci,oni->cn", w_down, pooled, preferred_element_type=jnp.float32
    ).astype(jnp.bfloat16)
    grad_down = jnp.einsum("cn,oni->oci", grad_coarse, pooled, preferred_element_type=jnp.float32)
    coarse_rows = grad_coarse.T
    padded_grad = jnp.concatenate(
        [coarse_rows, jnp.zeros((1, coarse_rows.shape[1]), jnp.bfloat16)], axis=0
    )
    returned = []
    for level in range(levels):
        coarse_index = jnp.where(
            got_keys[level] < sentinel, got_keys[level] % coarse_dev, coarse_dev
        )
        outbound = jnp.take(padded_grad, coarse_index, axis=0)
        if level < bits_member:
            returned.append(from_partner(outbound, "member", level))
        else:
            returned.append(from_partner(outbound, "group", level - bits_member))
    parent_table = jnp.concatenate([coarse_rows] + returned, axis=0)
    parent_index = jnp.where(is_self, coarse_id, coarse_dev + position)
    parents = jnp.take(parent_table, parent_index, axis=0)
    every = jnp.einsum("oci,vc->voi", w_down, parents, preferred_element_type=jnp.float32)
    chosen = (octant[:, None] == jnp.arange(noct, dtype=jnp.int32)[None, :]).astype(jnp.float32)
    grad_y1 = jnp.sum(every * chosen[:, :, None], axis=1).astype(jnp.bfloat16)
    sig = jax.nn.sigmoid(pre)
    grad_pre = (grad_y1.astype(jnp.float32) * (sig * (1.0 + pre * (1.0 - sig)))).astype(
        jnp.bfloat16
    )

    def backward_step(grad_table, inputs):
        weight, cols = inputs
        taken = jnp.take(table, cols, axis=0)
        dweight = lax.dot_general(
            grad_pre, taken, (((0,), (0,)), ((), ())), preferred_element_type=jnp.float32
        )
        contrib = jnp.dot(grad_pre, weight, preferred_element_type=jnp.float32)
        return (grad_table.at[cols].add(contrib), dweight)

    grad_table, grad_sub = lax.scan(
        backward_step, jnp.zeros((table.shape[0], chans), jnp.float32), (w_sub, kmap)
    )
    backs = [grad_table[vdev + level * hcap : vdev + (level + 1) * hcap] for level in range(levels)]
    incoming = []
    for level in range(levels):
        if level < bits_member:
            incoming.append(
                from_partner(backs[level].astype(jnp.bfloat16), "member", level).astype(jnp.float32)
            )
        else:
            incoming.append(
                from_partner(
                    backs[level].astype(jnp.bfloat16), "group", level - bits_member
                ).astype(jnp.float32)
            )
    grad_local = grad_table[:vdev]
    for level in range(levels):
        grad_local = grad_local.at[outgoing[level]].add(incoming[level])
    sub_total, down_total = lax.psum((grad_sub, grad_down), ("group", "member"))
    return (coarse_out, grad_local.T, sub_total, down_total)


def solution(mesh):
    in_specs = (
        P(None, ("group", "member")),
        P(None, ("group", "member")),
        P(("group", "member"), None, None),
        P(),
        P(("group", "member"), None),
        P(("group", "member")),
        P(("group", "member")),
        P(),
        P(None, ("group", "member")),
    )
    out_specs = (P(None, ("group", "member")), P(None, ("group", "member")), P(), P())
    return jax.shard_map(shards, mesh=mesh, in_specs=in_specs, out_specs=out_specs, check_vma=False)
```

profile of v0, /device:TPU:1, one launch (start us, length us, event | category | flops | bytes accessed | tf_op | source)
XLA Modules:
  0.0 2140.4 jit_solution(16183327324175720473)
XLA Ops:
  12.5 15.5 scatter_custom_fusion.1
  140.0 437.4 %while.24 = (s32[]{:T(128)}, f32[4096,96]{0,1:T(8,128)}, s32[27,4096]{1,0:T(8,128)}, bf16[5889,96]{1,0:T(8,128)(2,1)S(1)}, bf16[27,96,96]{2,1,0:T(8,128)(2,1)}, /*index=5*/s32[]{:T(128)}, s32[]{:T(128)}) while((s32[]{:T(128)}, f32[4096,96]{0,1:T(8,128)}, s32[27,4096]{1,0:T(8,128)}, bf16[5889,96]{1,0:T(8,128)(2,1)S(1)}, ...), condition=%wide.region_5.8_spmd.clone, body=%wide.region_4.7_spmd.clone.sunk | while | flops 76718080 | bytes 5636699 | solution.py:36
  586.5 17.1 gather_fusion.2
  635.4 1296.5 %while.23 = (s32[]{:T(128)}, f32[5889,96]{1,0:T(8,128)}, f32[27,96,96]{2,1,0:T(8,128)}, s32[27,4096]{1,0:T(8,128)}, bf16[27,96,96]{2,1,0:T(8,128)(2,1)}, /*index...) while((s32[]{:T(128)}, f32[5889,96]{1,0:T(8,128)}, f32[27,96,96]{2,1,0:T(8,128)}, ...), condition=%wide.region_11.15_spmd, body=%wide.region_9.14_spmd.sunk | while | flops 151834624 | bytes 20284560 | solution.py:111
  636.5 14.9 gather_fusion
  659.5 23.9 %scatter_fusion = f32[5889,96]{1,0:T(8,128)} fusion(f32[5889,96]{1,0:T(8,128)} %get-tuple-element.322, s32[4096]{0:T(1024)S(1)} %bitcast.141, f32[4096,96]{1,0:T(8,128)} %copy.63), kind=kCustom, calls=%fused_computation.17.clone.1 | custom fusion | flops 393216 | bytes 4734976 | tf_op jit(solution)/shard_map/while/body/eval_jaxpr/scatter-add | solution.py:109
  684.5 14.9 gather_fusion
  707.5 23.9 %scatter_fusion = f32[5889,96]{1,0:T(8,128)} fusion(f32[5889,96]{1,0:T(8,128)} %get-tuple-element.322, s32[4096]{0:T(1024)S(1)} %bitcast.141, f32[4096,96]{1,0:T(8,128)} %copy.63), kind=kCustom, calls=%fused_computation.17.clone.1 | custom fusion | flops 393216 | bytes 4734976 | tf_op jit(solution)/shard_map/while/body/eval_jaxpr/scatter-add | solution.py:109
  755.5 23.9 %scatter_fusion = f32[5889,96]{1,0:T(8,128)} fusion(f32[5889,96]{1,0:T(8,128)} %get-tuple-element.322, s32[4096]{0:T(1024)S(1)} %bitcast.141, f32[4096,96]{1,0:T(8,128)} %copy.63), kind=kCustom, calls=%fused_computation.17.clone.1 | custom fusion | flops 393216 | bytes 4734976 | tf_op jit(solution)/shard_map/while/body/eval_jaxpr/scatter-add | solution.py:109
  803.5 24.0 %scatter_fusion = f32[5889,96]{1,0:T(8,128)} fusion(f32[5889,96]{1,0:T(8,128)} %get-tuple-element.322, s32[4096]{0:T(1024)S(1)} %bitcast.141, f32[4096,96]{1,0:T(8,128)} %copy.63), kind=kCustom, calls=%fused_computation.17.clone.1 | custom fusion | flops 393216 | bytes 4734976 | tf_op jit(solution)/shard_map/while/body/eval_jaxpr/scatter-add | solution.py:109
  828.6 14.9 gather_fusion
  851.6 23.9 %scatter_fusion = f32[5889,96]{1,0:T(8,128)} fusion(f32[5889,96]{1,0:T(8,128)} %get-tuple-element.322, s32[4096]{0:T(1024)S(1)} %bitcast.141, f32[4096,96]{1,0:T(8,128)} %copy.63), kind=kCustom, calls=%fused_computation.17.clone.1 | custom fusion | flops 393216 | bytes 4734976 | tf_op jit(solution)/shard_map/while/body/eval_jaxpr/scatter-add | solution.py:109
  876.6 14.9 gather_fusion
  899.6 23.9 %scatter_fusion = f32[5889,96]{1,0:T(8,128)} fusion(f32[5889,96]{1,0:T(8,128)} %get-tuple-element.322, s32[4096]{0:T(1024)S(1)} %bitcast.141, f32[4096,96]{1,0:T(8,128)} %copy.63), kind=kCustom, calls=%fused_computation.17.clone.1 | custom fusion | flops 393216 | bytes 4734976 | tf_op jit(solution)/shard_map/while/body/eval_jaxpr/scatter-add | solution.py:109
  947.6 23.9 %scatter_fusion = f32[5889,96]{1,0:T(8,128)} fusion(f32[5889,96]{1,0:T(8,128)} %get-tuple-element.322, s32[4096]{0:T(1024)S(1)} %bitcast.141, f32[4096,96]{1,0:T(8,128)} %copy.63), kind=kCustom, calls=%fused_computation.17.clone.1 | custom fusion | flops 393216 | bytes 4734976 | tf_op jit(solution)/shard_map/while/body/eval_jaxpr/scatter-add | solution.py:109
  972.6 14.9 gather_fusion
  995.6 23.9 %scatter_fusion = f32[5889,96]{1,0:T(8,128)} fusion(f32[5889,96]{1,0:T(8,128)} %get-tuple-element.322, s32[4096]{0:T(1024)S(1)} %bitcast.141, f32[4096,96]{1,0:T(8,128)} %copy.63), kind=kCustom, calls=%fused_computation.17.clone.1 | custom fusion | flops 393216 | bytes 4734976 | tf_op jit(solution)/shard_map/while/body/eval_jaxpr/scatter-add | solution.py:109
  1020.6 14.9 gather_fusion
  1043.6 24.0 %scatter_fusion = f32[5889,96]{1,0:T(8,128)} fusion(f32[5889,96]{1,0:T(8,128)} %get-tuple-element.322, s32[4096]{0:T(1024)S(1)} %bitcast.141, f32[4096,96]{1,0:T(8,128)} %copy.63), kind=kCustom, calls=%fused_computation.17.clone.1 | custom fusion | flops 393216 | bytes 4734976 | tf_op jit(solution)/shard_map/while/body/eval_jaxpr/scatter-add | solution.py:109
  1091.7 23.9 %scatter_fusion = f32[5889,96]{1,0:T(8,128)} fusion(f32[5889,96]{1,0:T(8,128)} %get-tuple-element.322, s32[4096]{0:T(1024)S(1)} %bitcast.141, f32[4096,96]{1,0:T(8,128)} %copy.63), kind=kCustom, calls=%fused_computation.17.clone.1 | custom fusion | flops 393216 | bytes 4734976 | tf_op jit(solution)/shard_map/while/body/eval_jaxpr/scatter-add | solution.py:109
  1116.7 14.9 gather_fusion
  1139.7 24.0 %scatter_fusion = f32[5889,96]{1,0:T(8,128)} fusion(f32[5889,96]{1,0:T(8,128)} %get-tuple-element.322, s32[4096]{0:T(1024)S(1)} %bitcast.141, f32[4096,96]{1,0:T(8,128)} %copy.63), kind=kCustom, calls=%fused_computation.17.clone.1 | custom fusion | flops 393216 | bytes 4734976 | tf_op jit(solution)/shard_map/while/body/eval_jaxpr/scatter-add | solution.py:109
  1187.7 23.9 %scatter_fusion = f32[5889,96]{1,0:T(8,128)} fusion(f32[5889,96]{1,0:T(8,128)} %get-tuple-element.322, s32[4096]{0:T(1024)S(1)} %bitcast.141, f32[4096,96]{1,0:T(8,128)} %copy.63), kind=kCustom, calls=%fused_computation.17.clone.1 | custom fusion | flops 393216 | bytes 4734976 | tf_op jit(solution)/shard_map/while/body/eval_jaxpr/scatter-add | solution.py:109
  1235.7 24.0 %scatter_fusion = f32[5889,96]{1,0:T(8,128)} fusion(f32[5889,96]{1,0:T(8,128)} %get-tuple-element.322, s32[4096]{0:T(1024)S(1)} %bitcast.141, f32[4096,96]{1,0:T(8,128)} %copy.63), kind=kCustom, calls=%fused_computation.17.clone.1 | custom fusion | flops 393216 | bytes 4734976 | tf_op jit(solution)/shard_map/while/body/eval_jaxpr/scatter-add | solution.py:109
  1260.7 14.9 gather_fusion
  1283.7 23.9 %scatter_fusion = f32[5889,96]{1,0:T(8,128)} fusion(f32[5889,96]{1,0:T(8,128)} %get-tuple-element.322, s32[4096]{0:T(1024)S(1)} %bitcast.141, f32[4096,96]{1,0:T(8,128)} %copy.63), kind=kCustom, calls=%fused_computation.17.clone.1 | custom fusion | flops 393216 | bytes 4734976 | tf_op jit(solution)/shard_map/while/body/eval_jaxpr/scatter-add | solution.py:109
  1331.8 24.0 %scatter_fusion = f32[5889,96]{1,0:T(8,128)} fusion(f32[5889,96]{1,0:T(8,128)} %get-tuple-element.322, s32[4096]{0:T(1024)S(1)} %bitcast.141, f32[4096,96]{1,0:T(8,128)} %copy.63), kind=kCustom, calls=%fused_computation.17.clone.1 | custom fusion | flops 393216 | bytes 4734976 | tf_op jit(solution)/shard_map/while/body/eval_jaxpr/scatter-add | solution.py:109
  1356.8 14.9 gather_fusion
  1379.8 23.9 %scatter_fusion = f32[5889,96]{1,0:T(8,128)} fusion(f32[5889,96]{1,0:T(8,128)} %get-tuple-element.322, s32[4096]{0:T(1024)S(1)} %bitcast.141, f32[4096,96]{1,0:T(8,128)} %copy.63), kind=kCustom, calls=%fused_computation.17.clone.1 | custom fusion | flops 393216 | bytes 4734976 | tf_op jit(solution)/shard_map/while/body/eval_jaxpr/scatter-add | solution.py:109
  1427.8 24.0 %scatter_fusion = f32[5889,96]{1,0:T(8,128)} fusion(f32[5889,96]{1,0:T(8,128)} %get-tuple-element.322, s32[4096]{0:T(1024)S(1)} %bitcast.141, f32[4096,96]{1,0:T(8,128)} %copy.63), kind=kCustom, calls=%fused_computation.17.clone.1 | custom fusion | flops 393216 | bytes 4734976 | tf_op jit(solution)/shard_map/while/body/eval_jaxpr/scatter-add | solution.py:109
  1475.8 23.9 %scatter_fusion = f32[5889,96]{1,0:T(8,128)} fusion(f32[5889,96]{1,0:T(8,128)} %get-tuple-element.322, s32[4096]{0:T(1024)S(1)} %bitcast.141, f32[4096,96]{1,0:T(8,128)} %copy.63), kind=kCustom, calls=%fused_computation.17.clone.1 | custom fusion | flops 393216 | bytes 4734976 | tf_op jit(solution)/shard_map/while/body/eval_jaxpr/scatter-add | solution.py:109
  1500.8 14.9 gather_fusion
  1523.8 23.9 %scatter_fusion = f32[5889,96]{1,0:T(8,128)} fusion(f32[5889,96]{1,0:T(8,128)} %get-tuple-element.322, s32[4096]{0:T(1024)S(1)} %bitcast.141, f32[4096,96]{1,0:T(8,128)} %copy.63), kind=kCustom, calls=%fused_computation.17.clone.1 | custom fusion | flops 393216 | bytes 4734976 | tf_op jit(solution)/shard_map/while/body/eval_jaxpr/scatter-add | solution.py:109
  1548.9 14.9 gather_fusion
  1571.9 23.9 %scatter_fusion = f32[5889,96]{1,0:T(8,128)} fusion(f32[5889,96]{1,0:T(8,128)} %get-tuple-element.322, s32[4096]{0:T(1024)S(1)} %bitcast.141, f32[4096,96]{1,0:T(8,128)} %copy.63), kind=kCustom, calls=%fused_computation.17.clone.1 | custom fusion | flops 393216 | bytes 4734976 | tf_op jit(solution)/shard_map/while/body/eval_jaxpr/scatter-add | solution.py:109
  1596.9 14.9 gather_fusion
  1619.9 23.9 %scatter_fusion = f32[5889,96]{1,0:T(8,128)} fusion(f32[5889,96]{1,0:T(8,128)} %get-tuple-element.322, s32[4096]{0:T(1024)S(1)} %bitcast.141, f32[4096,96]{1,0:T(8,128)} %copy.63), kind=kCustom, calls=%fused_computation.17.clone.1 | custom fusion | flops 393216 | bytes 4734976 | tf_op jit(solution)/shard_map/while/body/eval_jaxpr/scatter-add | solution.py:109
  1667.9 23.9 %scatter_fusion = f32[5889,96]{1,0:T(8,128)} fusion(f32[5889,96]{1,0:T(8,128)} %get-tuple-element.322, s32[4096]{0:T(1024)S(1)} %bitcast.141, f32[4096,96]{1,0:T(8,128)} %copy.63), kind=kCustom, calls=%fused_computation.17.clone.1 | custom fusion | flops 393216 | bytes 4734976 | tf_op jit(solution)/shard_map/while/body/eval_jaxpr/scatter-add | solution.py:109
  1715.9 23.9 %scatter_fusion = f32[5889,96]{1,0:T(8,128)} fusion(f32[5889,96]{1,0:T(8,128)} %get-tuple-element.322, s32[4096]{0:T(1024)S(1)} %bitcast.141, f32[4096,96]{1,0:T(8,128)} %copy.63), kind=kCustom, calls=%fused_computation.17.clone.1 | custom fusion | flops 393216 | bytes 4734976 | tf_op jit(solution)/shard_map/while/body/eval_jaxpr/scatter-add | solution.py:109
  1740.9 14.9 gather_fusion
  1763.9 23.9 %scatter_fusion = f32[5889,96]{1,0:T(8,128)} fusion(f32[5889,96]{1,0:T(8,128)} %get-tuple-element.322, s32[4096]{0:T(1024)S(1)} %bitcast.141, f32[4096,96]{1,0:T(8,128)} %copy.63), kind=kCustom, calls=%fused_computation.17.clone.1 | custom fusion | flops 393216 | bytes 4734976 | tf_op jit(solution)/shard_map/while/body/eval_jaxpr/scatter-add | solution.py:109
  1789.0 14.9 gather_fusion
  1812.0 23.9 %scatter_fusion = f32[5889,96]{1,0:T(8,128)} fusion(f32[5889,96]{1,0:T(8,128)} %get-tuple-element.322, s32[4096]{0:T(1024)S(1)} %bitcast.141, f32[4096,96]{1,0:T(8,128)} %copy.63), kind=kCustom, calls=%fused_computation.17.clone.1 | custom fusion | flops 393216 | bytes 4734976 | tf_op jit(solution)/shard_map/while/body/eval_jaxpr/scatter-add | solution.py:109
  1837.0 14.9 gather_fusion
  1860.0 23.9 %scatter_fusion = f32[5889,96]{1,0:T(8,128)} fusion(f32[5889,96]{1,0:T(8,128)} %get-tuple-element.322, s32[4096]{0:T(1024)S(1)} %bitcast.141, f32[4096,96]{1,0:T(8,128)} %copy.63), kind=kCustom, calls=%fused_computation.17.clone.1 | custom fusion | flops 393216 | bytes 4734976 | tf_op jit(solution)/shard_map/while/body/eval_jaxpr/scatter-add | solution.py:109
  1908.0 23.9 %scatter_fusion = f32[5889,96]{1,0:T(8,128)} fusion(f32[5889,96]{1,0:T(8,128)} %get-tuple-element.322, s32[4096]{0:T(1024)S(1)} %bitcast.141, f32[4096,96]{1,0:T(8,128)} %copy.63), kind=kCustom, calls=%fused_computation.17.clone.1 | custom fusion | flops 393216 | bytes 4734976 | tf_op jit(solution)/shard_map/while/body/eval_jaxpr/scatter-add | solution.py:109
  1945.0 30.2 %scatter_custom_fusion.3 = f32[4097,96]{1,0:T(8,128)} fusion(s32[4992]{0:T(1024)} %fusion.43, f32[4992,96]{1,0:T(8,128)} %copy.40, f32[]{:T(128)} %constant.109.clone.1), kind=kCustom, calls=%fused_computation.67 | custom fusion | flops 479232 | bytes 1573760 | tf_op jit(solution)/shard_map/scatter-add | solution.py:70
  2034.3 95.4 %all-reduce.4.cloned.1.call-done = (f32[27,96,96]{2,1,0:T(8,128)}, f32[8,192,96]{1,2,0:T(8,128)}) async-done(((f32[27,96,96]{2,1,0:T(8,128)}, f32[8,192,96]{1,2,0:T(8,128)}), (f32[27,96,96]{2,1,0:T(8,128)}, f32[8,192,96]{1,2,0:T(8,128)})) %all-reduce.4.cloned.1.call-update) | async-done | bytes 1585168 | tf_op jit(solution)/shard_map/psum | solution.py:130
  (722 shorter events, 1095.2 us)
Async XLA Ops:
  7.2 42.4 %copy-start.11 = (s32[4096]{0:T(1024)S(1)}, s32[4096]{0:T(1024)}, u32[]{:S(2)}) copy-start(s32[4096]{0:T(1024)} %param.24) | copy-start | bytes 49156
  7.2 43.1 %copy-start.6 = (bf16[96,4096]{1,0:T(8,128)(2,1)S(1)}, bf16[96,4096]{1,0:T(8,128)(2,1)}, u32[]{:S(2)}) copy-start(bf16[96,4096]{1,0:T(8,128)(2,1)} %param.19) | copy-start | bytes 2359300
  7.2 2122.6 %all-reduce.4.cloned.1.call-start = ((), (), s32[]{:S(2)}) async-start(), calls=%async_computation | async-start | bytes 4227072 | tf_op jit(solution)/shard_map/psum | solution.py:130
  11.1 39.1 %copy-start.14 = (s32[4096,1]{0,1:T(1,128)}, s32[4096,1]{0,1:T(1,128)S(1)}, u32[]{:S(2)}) copy-start(s32[4096,1]{0,1:T(1,128)S(1)} %compare_select_fusion.4) | copy-start | bytes 49156
  28.6 44.8 %collective-permute-start.2 = (s32[128]{0:T(128)}, s32[128]{0:T(128)}, u32[]{:S(2)}, u32[]{:S(2)}) collective-permute-start(s32[128]{0:T(128)} %get-tuple-element.197), channel_id=1, source_target_pairs={{0,4},{1,5},{2,6},{3,7},{4,0},{5,1},{6,2},{7,3},{8,12},{9,13},{10,... | collective-permute-start | bytes 1544 | tf_op jit(solution)/shard_map/ppermute | solution.py:10
  31.1 46.5 %collective-permute-start.1 = (s32[128]{0:T(128)}, s32[128]{0:T(128)}, u32[]{:S(2)}, u32[]{:S(2)}) collective-permute-start(s32[128]{0:T(128)} %get-tuple-element.198), channel_id=1, source_target_pairs={{0,2},{1,3},{2,0},{3,1},{4,6},{5,7},{6,4},{7,5},{8,10},{9,11},{10,... | collective-permute-start | bytes 1544 | tf_op jit(solution)/shard_map/ppermute | solution.py:10
  33.8 45.4 %collective-permute-start = (s32[128]{0:T(128)}, s32[128]{0:T(128)}, u32[]{:S(2)}, u32[]{:S(2)}) collective-permute-start(s32[128]{0:T(128)} %get-tuple-element.199), channel_id=1, source_target_pairs={{0,1},{1,0},{2,3},{3,2},{4,5},{5,4},{6,7},{7,6},{8,9},{9,8},{10,11... | collective-permute-start | bytes 1544 | tf_op jit(solution)/shard_map/ppermute | solution.py:10
  34.1 48.0 %collective-permute-start.4 = (s32[128]{0:T(128)}, s32[128]{0:T(128)}, u32[]{:S(2)}, u32[]{:S(2)}) collective-permute-start(s32[128]{0:T(128)} %get-tuple-element.195), channel_id=1, source_target_pairs={{0,16},{16,0},{32,48},{48,32},{64,80},{80,64},{96,112},{112,96},{1... | collective-permute-start | bytes 1544 | tf_op jit(solution)/shard_map/ppermute | solution.py:10
  35.7 49.4 %collective-permute-start.3 = (s32[128]{0:T(128)}, s32[128]{0:T(128)}, u32[]{:S(2)}, u32[]{:S(2)}) collective-permute-start(s32[128]{0:T(128)} %get-tuple-element.196), channel_id=1, source_target_pairs={{0,8},{1,9},{2,10},{3,11},{4,12},{5,13},{6,14},{7,15},{8,0},{9,1},... | collective-permute-start | bytes 1544 | tf_op jit(solution)/shard_map/ppermute | solution.py:10
  73.4 13.5 collective-permute-start.6
  77.6 18.5 collective-permute-start.5
  79.2 39.5 %collective-permute-start.7 = (bf16[256,96]{1,0:T(8,128)(2,1)}, bf16[256,96]{1,0:T(8,128)(2,1)}, u32[]{:S(2)}, u32[]{:S(2)}) collective-permute-start(bf16[256,96]{1,0:T(8,128)(2,1)} %broadcast_select_fusion.13), channel_id=1, source_target_pairs={{0,1},{1,0},{2,3},{3,2},{4,5},{5,4},{6,7},{7,6},{8,9},{9,8},{10,11... | collective-permute-start | bytes 147464 | tf_op jit(solution)/shard_map/ppermute | solution.py:10
  82.1 38.5 %collective-permute-start.8 = (bf16[256,96]{1,0:T(8,128)(2,1)}, bf16[256,96]{1,0:T(8,128)(2,1)}, u32[]{:S(2)}, u32[]{:S(2)}) collective-permute-start(bf16[256,96]{1,0:T(8,128)(2,1)} %broadcast_select_fusion.12), channel_id=1, source_target_pairs={{0,2},{1,3},{2,0},{3,1},{4,6},{5,7},{6,4},{7,5},{8,10},{9,11},{10,... | collective-permute-start | bytes 147464 | tf_op jit(solution)/shard_map/ppermute | solution.py:10
  85.1 39.6 %collective-permute-start.9 = (bf16[256,96]{1,0:T(8,128)(2,1)}, bf16[256,96]{1,0:T(8,128)(2,1)}, u32[]{:S(2)}, u32[]{:S(2)}) collective-permute-start(bf16[256,96]{1,0:T(8,128)(2,1)} %broadcast_select_fusion.11), channel_id=1, source_target_pairs={{0,4},{1,5},{2,6},{3,7},{4,0},{5,1},{6,2},{7,3},{8,12},{9,13},{10,... | collective-permute-start | bytes 147464 | tf_op jit(solution)/shard_map/ppermute | solution.py:10
  86.9 39.0 %collective-permute-start.10 = (bf16[256,96]{1,0:T(8,128)(2,1)}, bf16[256,96]{1,0:T(8,128)(2,1)}, u32[]{:S(2)}, u32[]{:S(2)}) collective-permute-start(bf16[256,96]{1,0:T(8,128)(2,1)} %broadcast_select_fusion.10), channel_id=1, source_target_pairs={{0,8},{1,9},{2,10},{3,11},{4,12},{5,13},{6,14},{7,15},{8,0},{9,1},... | collective-permute-start | bytes 147464 | tf_op jit(solution)/shard_map/ppermute | solution.py:10
  96.0 32.5 %collective-permute-start.11 = (bf16[256,96]{1,0:T(8,128)(2,1)}, bf16[256,96]{1,0:T(8,128)(2,1)}, u32[]{:S(2)}, u32[]{:S(2)}) collective-permute-start(bf16[256,96]{1,0:T(8,128)(2,1)} %broadcast_select_fusion.9), channel_id=1, source_target_pairs={{0,16},{16,0},{32,48},{48,32},{64,80},{80,64},{96,112},{112,96},{1... | collective-permute-start | bytes 147464 | tf_op jit(solution)/shard_map/ppermute | solution.py:10
  118.7 14.1 collective-permute-start.12
  120.6 460.9 %collective-permute-start.22 = (bf16[128,192]{1,0:T(8,128)(2,1)}, bf16[128,192]{1,0:T(8,128)(2,1)}, u32[]{:S(2)}, u32[]{:S(2)}) collective-permute-start(bf16[128,192]{1,0:T(8,128)(2,1)} %broadcast_select_fusion.5), channel_id=1, source_target_pairs={{0,2},{1,3},{2,0},{3,1},{4,6},{5,7},{6,4},{7,5},{8,10},{9,11},{10,... | collective-permute-start | bytes 147464 | tf_op jit(solution)/shard_map/ppermute | solution.py:10
  124.7 455.6 %collective-permute-start.21 = (bf16[128,192]{1,0:T(8,128)(2,1)}, bf16[128,192]{1,0:T(8,128)(2,1)}, u32[]{:S(2)}, u32[]{:S(2)}) collective-permute-start(bf16[128,192]{1,0:T(8,128)(2,1)} %broadcast_select_fusion.6), channel_id=1, source_target_pairs={{0,1},{1,0},{2,3},{3,2},{4,5},{5,4},{6,7},{7,6},{8,9},{9,8},{10,11... | collective-permute-start | bytes 147464 | tf_op jit(solution)/shard_map/ppermute | solution.py:10
  125.9 458.0 %collective-permute-start.23 = (bf16[128,192]{1,0:T(8,128)(2,1)}, bf16[128,192]{1,0:T(8,128)(2,1)}, u32[]{:S(2)}, u32[]{:S(2)}) collective-permute-start(bf16[128,192]{1,0:T(8,128)(2,1)} %broadcast_select_fusion.4), channel_id=1, source_target_pairs={{0,4},{1,5},{2,6},{3,7},{4,0},{5,1},{6,2},{7,3},{8,12},{9,13},{10,... | collective-permute-start | bytes 147464 | tf_op jit(solution)/shard_map/ppermute | solution.py:10
  128.5 456.2 %collective-permute-start.24 = (bf16[128,192]{1,0:T(8,128)(2,1)}, bf16[128,192]{1,0:T(8,128)(2,1)}, u32[]{:S(2)}, u32[]{:S(2)}) collective-permute-start(bf16[128,192]{1,0:T(8,128)(2,1)} %broadcast_select_fusion.3), channel_id=1, source_target_pairs={{0,8},{1,9},{2,10},{3,11},{4,12},{5,13},{6,14},{7,15},{8,0},{9,1},... | collective-permute-start | bytes 147464 | tf_op jit(solution)/shard_map/ppermute | solution.py:10
  132.8 4.7 collective-permute-start.13
  137.5 448.1 %collective-permute-start.25 = (bf16[128,192]{1,0:T(8,128)(2,1)S(1)}, bf16[128,192]{1,0:T(8,128)(2,1)}, u32[]{:S(2)}, u32[]{:S(2)}) collective-permute-start(bf16[128,192]{1,0:T(8,128)(2,1)S(1)} %broadcast_select_fusion.2), channel_id=1, source_target_pairs={{0,16},{16,0},{32,48},{48,32},{64,80},{80,64},{96,112},{112,96},{1... | collective-permute-start | bytes 147464 | tf_op jit(solution)/shard_map/ppermute | solution.py:10
  580.2 6.2 collective-permute-start.26
  581.5 5.0 collective-permute-start.27
  632.2 1302.3 %collective-permute-start.14 = (bf16[128,96]{1,0:T(8,128)(2,1)S(1)}, bf16[128,96]{1,0:T(8,128)(2,1)S(1)}, u32[]{:S(2)}, u32[]{:S(2)}) collective-permute-start(bf16[128,96]{1,0:T(8,128)(2,1)S(1)} %get-tuple-element.178), channel_id=1, source_target_pairs={{0,1},{1,0},{2,3},{3,2},{4,5},{5,4},{6,7},{7,6},{8,9},{9,8},{10,11... | collective-permute-start | bytes 73736 | tf_op jit(solution)/shard_map/ppermute | solution.py:10
  803.5 24.0 %copy-start.2 = (bf16[4096,96]{1,0:T(8,128)(2,1)S(1)}, bf16[4096,96]{1,0:T(8,128)(2,1)}, u32[]{:S(2)}) copy-start(bf16[4096,96]{1,0:T(8,128)(2,1)} %copy-done.1) | copy-start | bytes 2359300 | tf_op jit(solution)/shard_map/while
  899.6 24.0 %copy-start.2 = (bf16[4096,96]{1,0:T(8,128)(2,1)S(1)}, bf16[4096,96]{1,0:T(8,128)(2,1)}, u32[]{:S(2)}) copy-start(bf16[4096,96]{1,0:T(8,128)(2,1)} %copy-done.1) | copy-start | bytes 2359300 | tf_op jit(solution)/shard_map/while
  1043.6 24.0 %copy-start.2 = (bf16[4096,96]{1,0:T(8,128)(2,1)S(1)}, bf16[4096,96]{1,0:T(8,128)(2,1)}, u32[]{:S(2)}) copy-start(bf16[4096,96]{1,0:T(8,128)(2,1)} %copy-done.1) | copy-start | bytes 2359300 | tf_op jit(solution)/shard_map/while
  1091.7 24.0 %copy-start.2 = (bf16[4096,96]{1,0:T(8,128)(2,1)S(1)}, bf16[4096,96]{1,0:T(8,128)(2,1)}, u32[]{:S(2)}) copy-start(bf16[4096,96]{1,0:T(8,128)(2,1)} %copy-done.1) | copy-start | bytes 2359300 | tf_op jit(solution)/shard_map/while
  1139.7 24.0 %copy-start.2 = (bf16[4096,96]{1,0:T(8,128)(2,1)S(1)}, bf16[4096,96]{1,0:T(8,128)(2,1)}, u32[]{:S(2)}) copy-start(bf16[4096,96]{1,0:T(8,128)(2,1)} %copy-done.1) | copy-start | bytes 2359300 | tf_op jit(solution)/shard_map/while
  1235.7 24.0 %copy-start.2 = (bf16[4096,96]{1,0:T(8,128)(2,1)S(1)}, bf16[4096,96]{1,0:T(8,128)(2,1)}, u32[]{:S(2)}) copy-start(bf16[4096,96]{1,0:T(8,128)(2,1)} %copy-done.1) | copy-start | bytes 2359300 | tf_op jit(solution)/shard_map/while
  1331.8 24.0 %copy-start.2 = (bf16[4096,96]{1,0:T(8,128)(2,1)S(1)}, bf16[4096,96]{1,0:T(8,128)(2,1)}, u32[]{:S(2)}) copy-start(bf16[4096,96]{1,0:T(8,128)(2,1)} %copy-done.1) | copy-start | bytes 2359300 | tf_op jit(solution)/shard_map/while
  1427.8 24.0 %copy-start.2 = (bf16[4096,96]{1,0:T(8,128)(2,1)S(1)}, bf16[4096,96]{1,0:T(8,128)(2,1)}, u32[]{:S(2)}) copy-start(bf16[4096,96]{1,0:T(8,128)(2,1)} %copy-done.1) | copy-start | bytes 2359300 | tf_op jit(solution)/shard_map/while
  1763.9 24.0 %copy-start.2 = (bf16[4096,96]{1,0:T(8,128)(2,1)S(1)}, bf16[4096,96]{1,0:T(8,128)(2,1)}, u32[]{:S(2)}) copy-start(bf16[4096,96]{1,0:T(8,128)(2,1)} %copy-done.1) | copy-start | bytes 2359300 | tf_op jit(solution)/shard_map/while
  1931.9 4.4 collective-permute-start.15
  1932.4 6.1 collective-permute-start.16
  1932.4 6.8 collective-permute-start.17
  1932.6 7.4 collective-permute-start.18
  1934.5 6.2 collective-permute-start.19
  1936.3 5.2 collective-permute-start.20
  1980.4 14.2 collective-permute-start.28
  1981.3 13.9 collective-permute-start.29
  1987.2 20.7 collective-permute-start.30
  1988.3 24.4 %collective-permute-start.31 = (bf16[256,96]{1,0:T(8,128)(2,1)S(1)}, bf16[256,96]{1,0:T(8,128)(2,1)S(1)}, u32[]{:S(2)}, u32[]{:S(2)}) collective-permute-start(bf16[256,96]{1,0:T(8,128)(2,1)S(1)} %get-tuple-element.168), channel_id=1, source_target_pairs={{0,8},{1,9},{2,10},{3,11},{4,12},{5,13},{6,14},{7,15},{8,0},{9,1},... | collective-permute-start | bytes 147464 | tf_op jit(solution)/shard_map/ppermute | solution.py:10
  1992.2 25.2 %collective-permute-start.32 = (bf16[256,96]{1,0:T(8,128)(2,1)S(1)}, bf16[256,96]{1,0:T(8,128)(2,1)S(1)}, u32[]{:S(2)}, u32[]{:S(2)}) collective-permute-start(bf16[256,96]{1,0:T(8,128)(2,1)S(1)} %get-tuple-element.167), channel_id=1, source_target_pairs={{0,16},{16,0},{32,48},{48,32},{64,80},{80,64},{96,112},{112,96},{1... | collective-permute-start | bytes 147464 | tf_op jit(solution)/shard_map/ppermute | solution.py:10
  1994.6 27.5 %collective-permute-start.33 = (bf16[256,96]{1,0:T(8,128)(2,1)S(1)}, bf16[256,96]{1,0:T(8,128)(2,1)S(1)}, u32[]{:S(2)}, u32[]{:S(2)}) collective-permute-start(bf16[256,96]{1,0:T(8,128)(2,1)S(1)} %get-tuple-element.166), channel_id=1, source_target_pairs={{0,32},{16,48},{32,0},{48,16},{64,96},{80,112},{96,64},{112,80},{1... | collective-permute-start | bytes 147464 | tf_op jit(solution)/shard_map/ppermute | solution.py:10
  1995.2 31.7 %collective-permute-start.34 = (bf16[256,96]{1,0:T(8,128)(2,1)S(1)}, bf16[256,96]{1,0:T(8,128)(2,1)S(1)}, u32[]{:S(2)}, u32[]{:S(2)}) collective-permute-start(bf16[256,96]{1,0:T(8,128)(2,1)S(1)} %get-tuple-element.165), channel_id=1, source_target_pairs={{0,64},{16,80},{32,96},{48,112},{64,0},{80,16},{96,32},{112,48},{1... | collective-permute-start | bytes 147464 | tf_op jit(solution)/shard_map/ppermute | solution.py:10
  (59 other events, 940.0 us)
Sparse Core Ops, SparseCore 0:
  1978.4 151.3 all-reduce.3
where the time goes:
time: 2160 us; the launch traced here: 2140 us
  local copies, waits for them, and re-layouts  932 us (43%)
  other arithmetic  799 us (37%)
  matrix products  242 us (11%)
  waiting for transfers between devices  99.7 us (5%)
  starting transfers between devices  51.1 us (2%)
    scatter-add x27, other arithmetic, backward_step(): return (grad_table.at[cols].add(contrib), dweight)  647 us
    gather x27, local copies, waits for them, and re-layouts, backward_step(): taken = jnp.take(table, cols, axis=0)  403 us
    gather x27, local copies, waits for them, and re-layouts, forward_step(): taken = jnp.take(table, cols, axis=0)  327 us
    dot_general x27, matrix products, backward_step(): lax.dot_general(grad_pre, taken, (((0,), (0,)), ((), ())), preferred_elem...  102 us
    psum x1, waiting for transfers between devices, shards(): sub_total, down_total = lax.psum((grad_sub, grad_down), ('group', 'member'))  95.4 us
    dot_general x27, matrix products, forward_step(): jnp.dot(taken, weight.T, preferred_element_type=jnp.float32)  83.8 us
    ppermute x35, starting transfers between devices, from_partner(): return lax.ppermute(value, axis, pairs)  51 us
    dot_general x27, local copies, waits for them, and re-layouts, backward_step(): contrib = jnp.dot(grad_pre, weight, preferred_element_type=jnp.float32)  49.2 us
  transfers between devices with their start and end apart: 36, of which 2 were waited for; matrix products, arithmetic and copies ran while one was open for 87% of the time, Pallas kernels for 0%

commit v1 on v0

--- a/solution.py
+++ b/solution.py
@@ -127,7 +127,7 @@
     grad_local = grad_table[:vdev]
     for level in range(levels):
         grad_local = grad_local.at[outgoing[level]].add(incoming[level])
-    sub_total, down_total = lax.psum((grad_sub, grad_down), ("group", "member"))
+    sub_total, down_total = lax.psum(lax.psum((grad_sub, grad_down), "group"), "member")
     return (coarse_out, grad_local.T, sub_total, down_total)
 
 

time: 2160 us -> 2160 us (level)
    psum x1 -> x2, waiting for transfers between devices: 95.4 us -> 115 us  [the longest x1 64.3 us: shards(): lax.psum((grad_sub, grad_down), 'group')]
  transfers between devices with their start and end apart: 36 -> 37, of which waited for: 2 -> 3; matrix products, arithmetic and copies ran while one was open for 87% -> 86% of each run, Pallas kernels for 0% -> 0%
where the time goes in v1:
time: 2160 us; the launch traced here: 2150 us
  local copies, waits for them, and re-layouts  931 us (43%)
  other arithmetic  784 us (36%)
  matrix products  242 us (11%)
  waiting for transfers between devices  120 us (6%)
  starting transfers between devices  51.7 us (2%)
    scatter-add x27, other arithmetic, backward_step(): return (grad_table.at[cols].add(contrib), dweight)  646 us
    gather x27, local copies, waits for them, and re-layouts, backward_step(): taken = jnp.take(table, cols, axis=0)  402 us
    gather x27, local copies, waits for them, and re-layouts, forward_step(): taken = jnp.take(table, cols, axis=0)  328 us
    dot_general x27, matrix products, backward_step(): lax.dot_general(grad_pre, taken, (((0,), (0,)), ((), ())), preferred_elem...  102 us
    dot_general x27, matrix products, forward_step(): jnp.dot(taken, weight.T, preferred_element_type=jnp.float32)  84 us
    psum x1, waiting for transfers between devices, shards(): lax.psum((grad_sub, grad_down), 'group')  64.3 us
    ppermute x35, starting transfers between devices, from_partner(): return lax.ppermute(value, axis, pairs)  51.6 us
    psum x1, waiting for transfers between devices, shards(): lax.psum(lax.psum((grad_sub, grad_down), 'group'), 'member')  51 us
  transfers between devices with their start and end apart: 37, of which 3 were waited for; matrix products, arithmetic and copies ran while one was open for 86% of the time, Pallas kernels for 0%

profile of v1, /device:TPU:1, one launch (start us, length us, event | category | flops | bytes accessed | tf_op | source)
XLA Modules:
  0.0 2145.2 jit_solution(4443391319731863494)
XLA Ops:
  12.5 15.5 scatter_custom_fusion.1
  139.9 437.6 %while.24 = (s32[]{:T(128)}, f32[4096,96]{0,1:T(8,128)}, s32[27,4096]{1,0:T(8,128)}, bf16[5889,96]{1,0:T(8,128)(2,1)S(1)}, bf16[27,96,96]{2,1,0:T(8,128)(2,1)}, /*index=5*/s32[]{:T(128)}, s32[]{:T(128)}) while((s32[]{:T(128)}, f32[4096,96]{0,1:T(8,128)}, s32[27,4096]{1,0:T(8,128)}, bf16[5889,96]{1,0:T(8,128)(2,1)S(1)}, ...), condition=%wide.region_5.8_spmd.clone, body=%wide.region_4.7_spmd.clone.sunk | while | flops 76718080 | bytes 5636699 | solution.py:36
  586.5 17.1 gather_fusion.2
  635.5 1295.8 %while.23 = (s32[]{:T(128)}, f32[5889,96]{1,0:T(8,128)}, f32[27,96,96]{2,1,0:T(8,128)}, s32[27,4096]{1,0:T(8,128)}, bf16[27,96,96]{2,1,0:T(8,128)(2,1)}, /*index...) while((s32[]{:T(128)}, f32[5889,96]{1,0:T(8,128)}, f32[27,96,96]{2,1,0:T(8,128)}, ...), condition=%wide.region_11.15_spmd, body=%wide.region_9.14_spmd.sunk | while | flops 151834624 | bytes 20284560 | solution.py:111
  659.6 23.9 %scatter_fusion = f32[5889,96]{1,0:T(8,128)} fusion(f32[5889,96]{1,0:T(8,128)} %get-tuple-element.324, s32[4096]{0:T(1024)S(1)} %bitcast.141, f32[4096,96]{1,0:T(8,128)} %copy.63), kind=kCustom, calls=%fused_computation.17.clone.1 | custom fusion | flops 393216 | bytes 4734976 | tf_op jit(solution)/shard_map/while/body/eval_jaxpr/scatter-add | solution.py:109
  707.6 23.9 %scatter_fusion = f32[5889,96]{1,0:T(8,128)} fusion(f32[5889,96]{1,0:T(8,128)} %get-tuple-element.324, s32[4096]{0:T(1024)S(1)} %bitcast.141, f32[4096,96]{1,0:T(8,128)} %copy.63), kind=kCustom, calls=%fused_computation.17.clone.1 | custom fusion | flops 393216 | bytes 4734976 | tf_op jit(solution)/shard_map/while/body/eval_jaxpr/scatter-add | solution.py:109
  732.6 14.9 gather_fusion
  755.6 23.9 %scatter_fusion = f32[5889,96]{1,0:T(8,128)} fusion(f32[5889,96]{1,0:T(8,128)} %get-tuple-element.324, s32[4096]{0:T(1024)S(1)} %bitcast.141, f32[4096,96]{1,0:T(8,128)} %copy.63), kind=kCustom, calls=%fused_computation.17.clone.1 | custom fusion | flops 393216 | bytes 4734976 | tf_op jit(solution)/shard_map/while/body/eval_jaxpr/scatter-add | solution.py:109
  780.6 14.9 gather_fusion
  803.6 23.9 %scatter_fusion = f32[5889,96]{1,0:T(8,128)} fusion(f32[5889,96]{1,0:T(8,128)} %get-tuple-element.324, s32[4096]{0:T(1024)S(1)} %bitcast.141, f32[4096,96]{1,0:T(8,128)} %copy.63), kind=kCustom, calls=%fused_computation.17.clone.1 | custom fusion | flops 393216 | bytes 4734976 | tf_op jit(solution)/shard_map/while/body/eval_jaxpr/scatter-add | solution.py:109
  828.6 14.9 gather_fusion
  851.6 23.9 %scatter_fusion = f32[5889,96]{1,0:T(8,128)} fusion(f32[5889,96]{1,0:T(8,128)} %get-tuple-element.324, s32[4096]{0:T(1024)S(1)} %bitcast.141, f32[4096,96]{1,0:T(8,128)} %copy.63), kind=kCustom, calls=%fused_computation.17.clone.1 | custom fusion | flops 393216 | bytes 4734976 | tf_op jit(solution)/shard_map/while/body/eval_jaxpr/scatter-add | solution.py:109
  899.6 23.9 %scatter_fusion = f32[5889,96]{1,0:T(8,128)} fusion(f32[5889,96]{1,0:T(8,128)} %get-tuple-element.324, s32[4096]{0:T(1024)S(1)} %bitcast.141, f32[4096,96]{1,0:T(8,128)} %copy.63), kind=kCustom, calls=%fused_computation.17.clone.1 | custom fusion | flops 393216 | bytes 4734976 | tf_op jit(solution)/shard_map/while/body/eval_jaxpr/scatter-add | solution.py:109
  924.6 14.9 gather_fusion
  947.6 23.9 %scatter_fusion = f32[5889,96]{1,0:T(8,128)} fusion(f32[5889,96]{1,0:T(8,128)} %get-tuple-element.324, s32[4096]{0:T(1024)S(1)} %bitcast.141, f32[4096,96]{1,0:T(8,128)} %copy.63), kind=kCustom, calls=%fused_computation.17.clone.1 | custom fusion | flops 393216 | bytes 4734976 | tf_op jit(solution)/shard_map/while/body/eval_jaxpr/scatter-add | solution.py:109
  972.6 14.9 gather_fusion
  995.5 23.9 %scatter_fusion = f32[5889,96]{1,0:T(8,128)} fusion(f32[5889,96]{1,0:T(8,128)} %get-tuple-element.324, s32[4096]{0:T(1024)S(1)} %bitcast.141, f32[4096,96]{1,0:T(8,128)} %copy.63), kind=kCustom, calls=%fused_computation.17.clone.1 | custom fusion | flops 393216 | bytes 4734976 | tf_op jit(solution)/shard_map/while/body/eval_jaxpr/scatter-add | solution.py:109
  1020.5 14.9 gather_fusion
  1043.5 23.9 %scatter_fusion = f32[5889,96]{1,0:T(8,128)} fusion(f32[5889,96]{1,0:T(8,128)} %get-tuple-element.324, s32[4096]{0:T(1024)S(1)} %bitcast.141, f32[4096,96]{1,0:T(8,128)} %copy.63), kind=kCustom, calls=%fused_computation.17.clone.1 | custom fusion | flops 393216 | bytes 4734976 | tf_op jit(solution)/shard_map/while/body/eval_jaxpr/scatter-add | solution.py:109
  1068.5 14.9 gather_fusion
  1091.5 23.9 %scatter_fusion = f32[5889,96]{1,0:T(8,128)} fusion(f32[5889,96]{1,0:T(8,128)} %get-tuple-element.324, s32[4096]{0:T(1024)S(1)} %bitcast.141, f32[4096,96]{1,0:T(8,128)} %copy.63), kind=kCustom, calls=%fused_computation.17.clone.1 | custom fusion | flops 393216 | bytes 4734976 | tf_op jit(solution)/shard_map/while/body/eval_jaxpr/scatter-add | solution.py:109
  1116.5 14.9 gather_fusion
  1139.5 23.9 %scatter_fusion = f32[5889,96]{1,0:T(8,128)} fusion(f32[5889,96]{1,0:T(8,128)} %get-tuple-element.324, s32[4096]{0:T(1024)S(1)} %bitcast.141, f32[4096,96]{1,0:T(8,128)} %copy.63), kind=kCustom, calls=%fused_computation.17.clone.1 | custom fusion | flops 393216 | bytes 4734976 | tf_op jit(solution)/shard_map/while/body/eval_jaxpr/scatter-add | solution.py:109
  1187.5 23.9 %scatter_fusion = f32[5889,96]{1,0:T(8,128)} fusion(f32[5889,96]{1,0:T(8,128)} %get-tuple-element.324, s32[4096]{0:T(1024)S(1)} %bitcast.141, f32[4096,96]{1,0:T(8,128)} %copy.63), kind=kCustom, calls=%fused_computation.17.clone.1 | custom fusion | flops 393216 | bytes 4734976 | tf_op jit(solution)/shard_map/while/body/eval_jaxpr/scatter-add | solution.py:109
  1235.5 23.9 %scatter_fusion = f32[5889,96]{1,0:T(8,128)} fusion(f32[5889,96]{1,0:T(8,128)} %get-tuple-element.324, s32[4096]{0:T(1024)S(1)} %bitcast.141, f32[4096,96]{1,0:T(8,128)} %copy.63), kind=kCustom, calls=%fused_computation.17.clone.1 | custom fusion | flops 393216 | bytes 4734976 | tf_op jit(solution)/shard_map/while/body/eval_jaxpr/scatter-add | solution.py:109
  1283.5 23.9 %scatter_fusion = f32[5889,96]{1,0:T(8,128)} fusion(f32[5889,96]{1,0:T(8,128)} %get-tuple-element.324, s32[4096]{0:T(1024)S(1)} %bitcast.141, f32[4096,96]{1,0:T(8,128)} %copy.63), kind=kCustom, calls=%fused_computation.17.clone.1 | custom fusion | flops 393216 | bytes 4734976 | tf_op jit(solution)/shard_map/while/body/eval_jaxpr/scatter-add | solution.py:109
  1308.5 14.9 gather_fusion
  1331.5 23.9 %scatter_fusion = f32[5889,96]{1,0:T(8,128)} fusion(f32[5889,96]{1,0:T(8,128)} %get-tuple-element.324, s32[4096]{0:T(1024)S(1)} %bitcast.141, f32[4096,96]{1,0:T(8,128)} %copy.63), kind=kCustom, calls=%fused_computation.17.clone.1 | custom fusion | flops 393216 | bytes 4734976 | tf_op jit(solution)/shard_map/while/body/eval_jaxpr/scatter-add | solution.py:109
  1379.5 23.9 %scatter_fusion = f32[5889,96]{1,0:T(8,128)} fusion(f32[5889,96]{1,0:T(8,128)} %get-tuple-element.324, s32[4096]{0:T(1024)S(1)} %bitcast.141, f32[4096,96]{1,0:T(8,128)} %copy.63), kind=kCustom, calls=%fused_computation.17.clone.1 | custom fusion | flops 393216 | bytes 4734976 | tf_op jit(solution)/shard_map/while/body/eval_jaxpr/scatter-add | solution.py:109
  1404.5 14.9 gather_fusion
  1427.5 23.9 %scatter_fusion = f32[5889,96]{1,0:T(8,128)} fusion(f32[5889,96]{1,0:T(8,128)} %get-tuple-element.324, s32[4096]{0:T(1024)S(1)} %bitcast.141, f32[4096,96]{1,0:T(8,128)} %copy.63), kind=kCustom, calls=%fused_computation.17.clone.1 | custom fusion | flops 393216 | bytes 4734976 | tf_op jit(solution)/shard_map/while/body/eval_jaxpr/scatter-add | solution.py:109
  1452.5 14.9 gather_fusion
  1475.5 23.9 %scatter_fusion = f32[5889,96]{1,0:T(8,128)} fusion(f32[5889,96]{1,0:T(8,128)} %get-tuple-element.324, s32[4096]{0:T(1024)S(1)} %bitcast.141, f32[4096,96]{1,0:T(8,128)} %copy.63), kind=kCustom, calls=%fused_computation.17.clone.1 | custom fusion | flops 393216 | bytes 4734976 | tf_op jit(solution)/shard_map/while/body/eval_jaxpr/scatter-add | solution.py:109
  1500.5 14.9 gather_fusion
  1523.5 23.9 %scatter_fusion = f32[5889,96]{1,0:T(8,128)} fusion(f32[5889,96]{1,0:T(8,128)} %get-tuple-element.324, s32[4096]{0:T(1024)S(1)} %bitcast.141, f32[4096,96]{1,0:T(8,128)} %copy.63), kind=kCustom, calls=%fused_computation.17.clone.1 | custom fusion | flops 393216 | bytes 4734976 | tf_op jit(solution)/shard_map/while/body/eval_jaxpr/scatter-add | solution.py:109
  1571.5 23.9 %scatter_fusion = f32[5889,96]{1,0:T(8,128)} fusion(f32[5889,96]{1,0:T(8,128)} %get-tuple-element.324, s32[4096]{0:T(1024)S(1)} %bitcast.141, f32[4096,96]{1,0:T(8,128)} %copy.63), kind=kCustom, calls=%fused_computation.17.clone.1 | custom fusion | flops 393216 | bytes 4734976 | tf_op jit(solution)/shard_map/while/body/eval_jaxpr/scatter-add | solution.py:109
  1619.4 23.9 %scatter_fusion = f32[5889,96]{1,0:T(8,128)} fusion(f32[5889,96]{1,0:T(8,128)} %get-tuple-element.324, s32[4096]{0:T(1024)S(1)} %bitcast.141, f32[4096,96]{1,0:T(8,128)} %copy.63), kind=kCustom, calls=%fused_computation.17.clone.1 | custom fusion | flops 393216 | bytes 4734976 | tf_op jit(solution)/shard_map/while/body/eval_jaxpr/scatter-add | solution.py:109
  1667.4 23.9 %scatter_fusion = f32[5889,96]{1,0:T(8,128)} fusion(f32[5889,96]{1,0:T(8,128)} %get-tuple-element.324, s32[4096]{0:T(1024)S(1)} %bitcast.141, f32[4096,96]{1,0:T(8,128)} %copy.63), kind=kCustom, calls=%fused_computation.17.clone.1 | custom fusion | flops 393216 | bytes 4734976 | tf_op jit(solution)/shard_map/while/body/eval_jaxpr/scatter-add | solution.py:109
  1715.4 23.9 %scatter_fusion = f32[5889,96]{1,0:T(8,128)} fusion(f32[5889,96]{1,0:T(8,128)} %get-tuple-element.324, s32[4096]{0:T(1024)S(1)} %bitcast.141, f32[4096,96]{1,0:T(8,128)} %copy.63), kind=kCustom, calls=%fused_computation.17.clone.1 | custom fusion | flops 393216 | bytes 4734976 | tf_op jit(solution)/shard_map/while/body/eval_jaxpr/scatter-add | solution.py:109
  1740.4 14.9 gather_fusion
  1763.4 23.9 %scatter_fusion = f32[5889,96]{1,0:T(8,128)} fusion(f32[5889,96]{1,0:T(8,128)} %get-tuple-element.324, s32[4096]{0:T(1024)S(1)} %bitcast.141, f32[4096,96]{1,0:T(8,128)} %copy.63), kind=kCustom, calls=%fused_computation.17.clone.1 | custom fusion | flops 393216 | bytes 4734976 | tf_op jit(solution)/shard_map/while/body/eval_jaxpr/scatter-add | solution.py:109
  1811.4 23.9 %scatter_fusion = f32[5889,96]{1,0:T(8,128)} fusion(f32[5889,96]{1,0:T(8,128)} %get-tuple-element.324, s32[4096]{0:T(1024)S(1)} %bitcast.141, f32[4096,96]{1,0:T(8,128)} %copy.63), kind=kCustom, calls=%fused_computation.17.clone.1 | custom fusion | flops 393216 | bytes 4734976 | tf_op jit(solution)/shard_map/while/body/eval_jaxpr/scatter-add | solution.py:109
  1859.4 23.9 %scatter_fusion = f32[5889,96]{1,0:T(8,128)} fusion(f32[5889,96]{1,0:T(8,128)} %get-tuple-element.324, s32[4096]{0:T(1024)S(1)} %bitcast.141, f32[4096,96]{1,0:T(8,128)} %copy.63), kind=kCustom, calls=%fused_computation.17.clone.1 | custom fusion | flops 393216 | bytes 4734976 | tf_op jit(solution)/shard_map/while/body/eval_jaxpr/scatter-add | solution.py:109
  1884.4 14.9 gather_fusion
  1907.4 23.9 %scatter_fusion = f32[5889,96]{1,0:T(8,128)} fusion(f32[5889,96]{1,0:T(8,128)} %get-tuple-element.324, s32[4096]{0:T(1024)S(1)} %bitcast.141, f32[4096,96]{1,0:T(8,128)} %copy.63), kind=kCustom, calls=%fused_computation.17.clone.1 | custom fusion | flops 393216 | bytes 4734976 | tf_op jit(solution)/shard_map/while/body/eval_jaxpr/scatter-add | solution.py:109
  1944.4 29.2 %scatter_custom_fusion.3 = f32[4097,96]{1,0:T(8,128)S(1)} fusion(s32[4992]{0:T(1024)} %fusion.43, f32[4992,96]{1,0:T(8,128)} %copy.40, f32[]{:T(128)} %constant.109.clone.1), kind=kCustom, calls=%fused_computation.67 | custom fusion | flops 479232 | bytes 1573760 | tf_op jit(solution)/shard_map/scatter-add | solution.py:70
  1976.2 64.3 %all-reduce.8.cloned.1.call-done = (f32[27,96,96]{2,1,0:T(8,128)}, f32[8,192,96]{1,2,0:T(8,128)}) async-done(((f32[27,96,96]{2,1,0:T(8,128)}, f32[8,192,96]{1,2,0:T(8,128)}), (f32[27,96,96]{2,1,0:T(8,128)}, f32[8,192,96]{1,2,0:T(8,128)})) %all-reduce.8.cloned.1.call-update) | async-done | bytes 1585168 | tf_op jit(solution)/shard_map/psum | solution.py:130
  2083.6 51.0 %all-reduce.6.cloned.1.call-done = (f32[27,96,96]{2,1,0:T(8,128)}, f32[8,192,96]{1,2,0:T(8,128)}) async-done(((f32[27,96,96]{2,1,0:T(8,128)}, f32[8,192,96]{1,2,0:T(8,128)}), (f32[27,96,96]{2,1,0:T(8,128)}, f32[8,192,96]{1,2,0:T(8,128)})) %all-reduce.6.cloned.1.call-update) | async-done | bytes 1585168 | tf_op jit(solution)/shard_map/psum | solution.py:130
  (737 shorter events, 1096.6 us)
Async XLA Ops:
  7.2 42.4 %copy-start.17 = (s32[4096]{0:T(1024)S(1)}, s32[4096]{0:T(1024)}, u32[]{:S(2)}) copy-start(s32[4096]{0:T(1024)} %param.24) | copy-start | bytes 49156
  7.2 43.0 %copy-start.10 = (bf16[96,4096]{1,0:T(8,128)(2,1)S(1)}, bf16[96,4096]{1,0:T(8,128)(2,1)}, u32[]{:S(2)}) copy-start(bf16[96,4096]{1,0:T(8,128)(2,1)} %param.19) | copy-start | bytes 2359300
  7.2 2033.2 %all-reduce.8.cloned.1.call-start = ((), (), s32[]{:S(2)}) async-start(), calls=%async_computation.1 | async-start | bytes 4227072 | tf_op jit(solution)/shard_map/psum | solution.py:130
  11.1 38.4 %copy-start.20 = (s32[4096,1]{0,1:T(1,128)}, s32[4096,1]{0,1:T(1,128)S(1)}, u32[]{:S(2)}) copy-start(s32[4096,1]{0,1:T(1,128)S(1)} %compare_select_fusion.4) | copy-start | bytes 49156
  28.6 44.6 %collective-permute-start.2 = (s32[128]{0:T(128)}, s32[128]{0:T(128)}, u32[]{:S(2)}, u32[]{:S(2)}) collective-permute-start(s32[128]{0:T(128)} %get-tuple-element.199), channel_id=1, source_target_pairs={{0,4},{1,5},{2,6},{3,7},{4,0},{5,1},{6,2},{7,3},{8,12},{9,13},{10,... | collective-permute-start | bytes 1544 | tf_op jit(solution)/shard_map/ppermute | solution.py:10
  31.1 46.4 %collective-permute-start.1 = (s32[128]{0:T(128)}, s32[128]{0:T(128)}, u32[]{:S(2)}, u32[]{:S(2)}) collective-permute-start(s32[128]{0:T(128)} %get-tuple-element.200), channel_id=1, source_target_pairs={{0,2},{1,3},{2,0},{3,1},{4,6},{5,7},{6,4},{7,5},{8,10},{9,11},{10,... | collective-permute-start | bytes 1544 | tf_op jit(solution)/shard_map/ppermute | solution.py:10
  33.8 45.1 %collective-permute-start = (s32[128]{0:T(128)}, s32[128]{0:T(128)}, u32[]{:S(2)}, u32[]{:S(2)}) collective-permute-start(s32[128]{0:T(128)} %get-tuple-element.201), channel_id=1, source_target_pairs={{0,1},{1,0},{2,3},{3,2},{4,5},{5,4},{6,7},{7,6},{8,9},{9,8},{10,11... | collective-permute-start | bytes 1544 | tf_op jit(solution)/shard_map/ppermute | solution.py:10
  34.2 47.8 %collective-permute-start.4 = (s32[128]{0:T(128)}, s32[128]{0:T(128)}, u32[]{:S(2)}, u32[]{:S(2)}) collective-permute-start(s32[128]{0:T(128)} %get-tuple-element.197), channel_id=1, source_target_pairs={{0,16},{16,0},{32,48},{48,32},{64,80},{80,64},{96,112},{112,96},{1... | collective-permute-start | bytes 1544 | tf_op jit(solution)/shard_map/ppermute | solution.py:10
  35.7 49.3 %collective-permute-start.3 = (s32[128]{0:T(128)}, s32[128]{0:T(128)}, u32[]{:S(2)}, u32[]{:S(2)}) collective-permute-start(s32[128]{0:T(128)} %get-tuple-element.198), channel_id=1, source_target_pairs={{0,8},{1,9},{2,10},{3,11},{4,12},{5,13},{6,14},{7,15},{8,0},{9,1},... | collective-permute-start | bytes 1544 | tf_op jit(solution)/shard_map/ppermute | solution.py:10
  73.2 13.5 collective-permute-start.6
  77.5 18.4 collective-permute-start.5
  78.9 39.6 %collective-permute-start.7 = (bf16[256,96]{1,0:T(8,128)(2,1)}, bf16[256,96]{1,0:T(8,128)(2,1)}, u32[]{:S(2)}, u32[]{:S(2)}) collective-permute-start(bf16[256,96]{1,0:T(8,128)(2,1)} %broadcast_select_fusion.13), channel_id=1, source_target_pairs={{0,1},{1,0},{2,3},{3,2},{4,5},{5,4},{6,7},{7,6},{8,9},{9,8},{10,11... | collective-permute-start | bytes 147464 | tf_op jit(solution)/shard_map/ppermute | solution.py:10
  82.0 38.4 %collective-permute-start.8 = (bf16[256,96]{1,0:T(8,128)(2,1)}, bf16[256,96]{1,0:T(8,128)(2,1)}, u32[]{:S(2)}, u32[]{:S(2)}) collective-permute-start(bf16[256,96]{1,0:T(8,128)(2,1)} %broadcast_select_fusion.12), channel_id=1, source_target_pairs={{0,2},{1,3},{2,0},{3,1},{4,6},{5,7},{6,4},{7,5},{8,10},{9,11},{10,... | collective-permute-start | bytes 147464 | tf_op jit(solution)/shard_map/ppermute | solution.py:10
  85.0 39.5 %collective-permute-start.9 = (bf16[256,96]{1,0:T(8,128)(2,1)}, bf16[256,96]{1,0:T(8,128)(2,1)}, u32[]{:S(2)}, u32[]{:S(2)}) collective-permute-start(bf16[256,96]{1,0:T(8,128)(2,1)} %broadcast_select_fusion.11), channel_id=1, source_target_pairs={{0,4},{1,5},{2,6},{3,7},{4,0},{5,1},{6,2},{7,3},{8,12},{9,13},{10,... | collective-permute-start | bytes 147464 | tf_op jit(solution)/shard_map/ppermute | solution.py:10
  86.7 39.0 %collective-permute-start.10 = (bf16[256,96]{1,0:T(8,128)(2,1)}, bf16[256,96]{1,0:T(8,128)(2,1)}, u32[]{:S(2)}, u32[]{:S(2)}) collective-permute-start(bf16[256,96]{1,0:T(8,128)(2,1)} %broadcast_select_fusion.10), channel_id=1, source_target_pairs={{0,8},{1,9},{2,10},{3,11},{4,12},{5,13},{6,14},{7,15},{8,0},{9,1},... | collective-permute-start | bytes 147464 | tf_op jit(solution)/shard_map/ppermute | solution.py:10
  95.8 32.5 %collective-permute-start.11 = (bf16[256,96]{1,0:T(8,128)(2,1)}, bf16[256,96]{1,0:T(8,128)(2,1)}, u32[]{:S(2)}, u32[]{:S(2)}) collective-permute-start(bf16[256,96]{1,0:T(8,128)(2,1)} %broadcast_select_fusion.9), channel_id=1, source_target_pairs={{0,16},{16,0},{32,48},{48,32},{64,80},{80,64},{96,112},{112,96},{1... | collective-permute-start | bytes 147464 | tf_op jit(solution)/shard_map/ppermute | solution.py:10
  118.5 14.1 collective-permute-start.12
  120.4 461.1 %collective-permute-start.22 = (bf16[128,192]{1,0:T(8,128)(2,1)}, bf16[128,192]{1,0:T(8,128)(2,1)}, u32[]{:S(2)}, u32[]{:S(2)}) collective-permute-start(bf16[128,192]{1,0:T(8,128)(2,1)} %broadcast_select_fusion.5), channel_id=1, source_target_pairs={{0,2},{1,3},{2,0},{3,1},{4,6},{5,7},{6,4},{7,5},{8,10},{9,11},{10,... | collective-permute-start | bytes 147464 | tf_op jit(solution)/shard_map/ppermute | solution.py:10
  124.5 455.7 %collective-permute-start.21 = (bf16[128,192]{1,0:T(8,128)(2,1)}, bf16[128,192]{1,0:T(8,128)(2,1)}, u32[]{:S(2)}, u32[]{:S(2)}) collective-permute-start(bf16[128,192]{1,0:T(8,128)(2,1)} %broadcast_select_fusion.6), channel_id=1, source_target_pairs={{0,1},{1,0},{2,3},{3,2},{4,5},{5,4},{6,7},{7,6},{8,9},{9,8},{10,11... | collective-permute-start | bytes 147464 | tf_op jit(solution)/shard_map/ppermute | solution.py:10
  125.8 458.1 %collective-permute-start.23 = (bf16[128,192]{1,0:T(8,128)(2,1)}, bf16[128,192]{1,0:T(8,128)(2,1)}, u32[]{:S(2)}, u32[]{:S(2)}) collective-permute-start(bf16[128,192]{1,0:T(8,128)(2,1)} %broadcast_select_fusion.4), channel_id=1, source_target_pairs={{0,4},{1,5},{2,6},{3,7},{4,0},{5,1},{6,2},{7,3},{8,12},{9,13},{10,... | collective-permute-start | bytes 147464 | tf_op jit(solution)/shard_map/ppermute | solution.py:10
  128.4 456.4 %collective-permute-start.24 = (bf16[128,192]{1,0:T(8,128)(2,1)}, bf16[128,192]{1,0:T(8,128)(2,1)}, u32[]{:S(2)}, u32[]{:S(2)}) collective-permute-start(bf16[128,192]{1,0:T(8,128)(2,1)} %broadcast_select_fusion.3), channel_id=1, source_target_pairs={{0,8},{1,9},{2,10},{3,11},{4,12},{5,13},{6,14},{7,15},{8,0},{9,1},... | collective-permute-start | bytes 147464 | tf_op jit(solution)/shard_map/ppermute | solution.py:10
  132.6 4.7 collective-permute-start.13
  137.3 448.3 %collective-permute-start.25 = (bf16[128,192]{1,0:T(8,128)(2,1)S(1)}, bf16[128,192]{1,0:T(8,128)(2,1)}, u32[]{:S(2)}, u32[]{:S(2)}) collective-permute-start(bf16[128,192]{1,0:T(8,128)(2,1)S(1)} %broadcast_select_fusion.2), channel_id=1, source_target_pairs={{0,16},{16,0},{32,48},{48,32},{64,80},{80,64},{96,112},{112,96},{1... | collective-permute-start | bytes 147464 | tf_op jit(solution)/shard_map/ppermute | solution.py:10
  580.2 6.2 collective-permute-start.26
  581.5 5.0 collective-permute-start.27
  632.4 1301.5 %collective-permute-start.14 = (bf16[128,96]{1,0:T(8,128)(2,1)S(1)}, bf16[128,96]{1,0:T(8,128)(2,1)S(1)}, u32[]{:S(2)}, u32[]{:S(2)}) collective-permute-start(bf16[128,96]{1,0:T(8,128)(2,1)S(1)} %get-tuple-element.180), channel_id=1, source_target_pairs={{0,1},{1,0},{2,3},{3,2},{4,5},{5,4},{6,7},{7,6},{8,9},{9,8},{10,11... | collective-permute-start | bytes 73736 | tf_op jit(solution)/shard_map/ppermute | solution.py:10
  803.6 23.9 %copy-start.3 = (bf16[4096,96]{1,0:T(8,128)(2,1)S(1)}, bf16[4096,96]{1,0:T(8,128)(2,1)}, u32[]{:S(2)}) copy-start(bf16[4096,96]{1,0:T(8,128)(2,1)} %copy-done.2) | copy-start | bytes 2359300 | tf_op jit(solution)/shard_map/while
  1043.5 23.9 %copy-start.3 = (bf16[4096,96]{1,0:T(8,128)(2,1)S(1)}, bf16[4096,96]{1,0:T(8,128)(2,1)}, u32[]{:S(2)}) copy-start(bf16[4096,96]{1,0:T(8,128)(2,1)} %copy-done.2) | copy-start | bytes 2359300 | tf_op jit(solution)/shard_map/while
  1139.5 23.9 %copy-start.3 = (bf16[4096,96]{1,0:T(8,128)(2,1)S(1)}, bf16[4096,96]{1,0:T(8,128)(2,1)}, u32[]{:S(2)}) copy-start(bf16[4096,96]{1,0:T(8,128)(2,1)} %copy-done.2) | copy-start | bytes 2359300 | tf_op jit(solution)/shard_map/while
  1235.5 23.9 %copy-start.3 = (bf16[4096,96]{1,0:T(8,128)(2,1)S(1)}, bf16[4096,96]{1,0:T(8,128)(2,1)}, u32[]{:S(2)}) copy-start(bf16[4096,96]{1,0:T(8,128)(2,1)} %copy-done.2) | copy-start | bytes 2359300 | tf_op jit(solution)/shard_map/while
  1331.5 23.9 %copy-start.3 = (bf16[4096,96]{1,0:T(8,128)(2,1)S(1)}, bf16[4096,96]{1,0:T(8,128)(2,1)}, u32[]{:S(2)}) copy-start(bf16[4096,96]{1,0:T(8,128)(2,1)} %copy-done.2) | copy-start | bytes 2359300 | tf_op jit(solution)/shard_map/while
  1427.5 23.9 %copy-start.3 = (bf16[4096,96]{1,0:T(8,128)(2,1)S(1)}, bf16[4096,96]{1,0:T(8,128)(2,1)}, u32[]{:S(2)}) copy-start(bf16[4096,96]{1,0:T(8,128)(2,1)} %copy-done.2) | copy-start | bytes 2359300 | tf_op jit(solution)/shard_map/while
  1763.4 23.9 %copy-start.3 = (bf16[4096,96]{1,0:T(8,128)(2,1)S(1)}, bf16[4096,96]{1,0:T(8,128)(2,1)}, u32[]{:S(2)}) copy-start(bf16[4096,96]{1,0:T(8,128)(2,1)} %copy-done.2) | copy-start | bytes 2359300 | tf_op jit(solution)/shard_map/while
  1931.3 4.4 collective-permute-start.15
  1931.9 6.1 collective-permute-start.16
  1931.9 6.8 collective-permute-start.17
  1932.0 7.5 collective-permute-start.18
  1933.9 6.3 collective-permute-start.19
  1935.7 5.2 collective-permute-start.20
  1976.1 64.4 %copy-start = (f32[5889,96]{1,0:T(8,128)S(1)}, f32[5889,96]{1,0:T(8,128)}, u32[]{:S(2)}) copy-start(f32[5889,96]{1,0:T(8,128)} %get-tuple-element.73) | copy-start | bytes 6784132
  1976.1 158.5 %all-reduce.6.cloned.1.call-start = ((), (), s32[]{:S(2)}) async-start(), calls=%async_computation | async-start | bytes 4227072 | tf_op jit(solution)/shard_map/psum | solution.py:130
  2041.4 16.4 collective-permute-start.28
  2042.5 15.5 collective-permute-start.29
  2048.1 18.6 collective-permute-start.30
  2049.4 20.4 collective-permute-start.31
  2052.0 20.8 collective-permute-start.32
  2057.8 18.1 collective-permute-start.33
  2058.1 20.8 collective-permute-start.34
  (66 other events, 1014.2 us)
Sparse Core Ops, SparseCore 0:
  1976.2 64.1 all-reduce.7
  2043.9 90.6 all-reduce.5
